TPU v7x, 32 devices: a whole 2x2x4 slice. The times are simulated.
32 devices in a mesh: mem: 4 (over z), tile: 8 (over y, x, core).
Axes of the slice: x: 2, y: 2, z: 4, core: 2. Of those that a mesh axis runs over, the one named last changes fastest.
Arguments:
- alpha: float32 [32, 8, 192, 384], P('mem', None, 'tile'), may hold values from -6 to 6
- ensemble: bfloat16 [2, 32, 8, 192, 384], P(None, 'mem', None, 'tile'), may hold values from -1 to 1
- innovation: float32 [2, 8, 192, 384], P(None, None, 'tile'), may hold values from -6 to 6
- precision: float32 [2, 8, 192, 384], P(None, None, 'tile'), may hold values from 0.5 to 8
- diffusivity: float32 [2, 8, 192, 384], P(None, None, 'tile'), may hold values from 0.01 to 0.48, as said below
Outputs:
- gradient: float32 [32, 8, 192, 384], P('mem', None, 'tile')
- increment: float32 [2, 8, 192, 384], P(None, None, 'tile')
Inputs may be any that keep to these rules, and one draw needn't show every extreme that they name: diffusivity[0] lies between 0.40 and 0.48 and diffusivity[1] between 0.01 and 0.02, so the four faces of a cell sum to at most 1.
All inputs are finite; a program needn't handle non-finite values.
Results may differ from a plain program's by a relative error of at most 0.0003.
Values sent between devices are 32-bit elements; how exact they have to be, the bound alone decides.
A program may use at most 64 MiB of HBM per device.

v0:
```python
import jax
import jax.numpy as jnp
from jax import lax
from jax.sharding import PartitionSpec as P

STEPS = 4


def extended(cells, sides, width):
    for axis, dim in sides:
        count = lax.axis_size(axis)
        head = lax.slice_in_dim(cells, 0, width, axis=dim)
        tail = lax.slice_in_dim(cells, cells.shape[dim] - width, cells.shape[dim], axis=dim)
        cells = jnp.concatenate(
            [
                lax.ppermute(tail, axis, [(i, (i + 1) % count) for i in range(count)]),
                cells,
                lax.ppermute(head, axis, [((i + 1) % count, i) for i in range(count)]),
            ],
            axis=dim,
        )
    return cells


def diffuse(field, coeffs, width):
    for sweep in range(width):
        columns = field.shape[2]
        zonal_face = coeffs[0, :, sweep : sweep + columns - 1]
        merid_face = coeffs[1, :, sweep + 1 : sweep + columns - 1]
        zonal_flux = zonal_face * (field[:, :, 1:] - field[:, :, :-1])
        interior = field[:, :, 1:-1]
        merid_flux = merid_face[:, :, :-1] * (interior[:, :, :, 1:] - interior[:, :, :, :-1])
        padding = jnp.zeros_like(interior[:, :, :, :1])
        north_flux = jnp.concatenate([merid_flux, padding], axis=3)
        south_flux = jnp.concatenate([padding, merid_flux], axis=3)
        field = interior + zonal_flux[:, :, 1:] - zonal_flux[:, :, :-1] + north_flux - south_flux
    return field


def per_device(alpha, ensemble, innovation, precision, diffusivity):
    coeffs = extended(diffusivity, (("tile", 2),), STEPS)
    padded = extended(alpha, (("tile", 2),), STEPS)
    localized = diffuse(padded, coeffs, STEPS)
    partial_sum = jnp.sum(ensemble.astype(jnp.float32) * localized[None], axis=1)
    increment = lax.psum(partial_sum, "mem")
    weighted = precision * (increment - innovation)
    projected = jnp.sum(ensemble.astype(jnp.float32) * weighted[:, None], axis=0)
    padded_adj = extended(projected, (("tile", 2),), STEPS)
    adjoint_field = diffuse(padded_adj, coeffs, STEPS)
    gradient = alpha + adjoint_field
    return (gradient, increment)


def solution(mesh):
    in_specs = (
        P("mem", None, "tile", None),
        P(None, "mem", None, "tile", None),
        P(None, None, "tile", None),
        P(None, None, "tile", None),
        P(None, None, "tile", None),
    )
    out_specs = (P("mem", None, "tile", None), P(None, None, "tile", None))
    return jax.shard_map(
        per_device, mesh=mesh, in_specs=in_specs, out_specs=out_specs, check_vma=False
    )
```

profile of v0, /device:TPU:0, one launch (start us, length us, event | category | flops | bytes accessed | tf_op | source)
XLA Modules:
  0.0 120.2 jit_solution(3033836365526358352)
XLA Ops:
  7.2 1.1 fusion.38
  8.9 2.9 %collective-permute-start.3 = (f32[2,8,4,384]{3,2,1,0:T(4,128)S(1)}, f32[2,8,4,384]{3,2,1,0:T(4,128)S(1)}, u32[]{:S(2)}, u32[]{:S(2)}) collective-permute-start(f32[2,8,4,384]{3,2,1,0:T(4,128)S(1)} %get-tuple-element.9), channel_id=1, source_target_pairs={{1,0},{2,1},{3,2},{4,3},{5,4},{6,5},{7,6},{0,7},{9,8},{10,9},{11,1... | collective-permute-start | bytes 294920 | tf_op jit(solution)/shard_map/ppermute | solution.py:18
  11.8 1.5 %fusion.37 = (f32[8,8,4,384]{3,2,1,0:T(4,128)S(1)}, f32[8,8,4,384]{3,2,1,0:T(4,128)S(1)}) fusion(f32[8,8,24,384]{3,2,1,0:T(8,128)} %param.5), kind=kLoop, calls=%fused_computation.83 | loop fusion | bytes 1572864 | tf_op jit(solution)/shard_map/slice | solution.py:13
  13.5 2.7 %collective-permute-start.1 = (f32[8,8,4,384]{3,1,2,0:T(8,128)S(1)}, f32[8,8,4,384]{3,1,2,0:T(8,128)S(1)}, u32[]{:S(2)}, u32[]{:S(2)}) collective-permute-start(f32[8,8,4,384]{3,1,2,0:T(8,128)S(1)} %copy.30), channel_id=1, source_target_pairs={{1,0},{2,1},{3,2},{4,3},{5,4},{6,5},{7,6},{0,7},{9,8},{10,9},{11,1... | collective-permute-start | bytes 1179656 | tf_op jit(solution)/shard_map/ppermute | solution.py:18
  16.2 0.8 slice_bitcast_fusion.6
  17.1 0.8 slice_bitcast_fusion.2
  17.9 0.8 slice_bitcast_fusion.3
  18.7 0.8 slice_bitcast_fusion
  19.5 0.8 slice_bitcast_fusion.1
  20.3 3.7 %collective-permute-done = f32[8,8,4,384]{3,1,2,0:T(8,128)S(1)} collective-permute-done((f32[8,8,4,384]{3,1,2,0:T(8,128)S(1)}, f32[8,8,4,384]{3,1,2,0:T(8,128)S(1)}, u32[]{:S(2)}, u32[]{:S(2)}) %collective-permute-start) | collective-permute-done | bytes 393248 | tf_op jit(solution)/shard_map/ppermute | solution.py:16
  24.8 1.2 fusion.24
  26.5 1.7 %fusion.26 = f32[8,8,30,384]{3,2,1,0:T(8,128)S(1)} fusion(f32[8,8,31,384]{3,2,1,0:T(8,128)S(1)} %fusion.27, f32[8,8,32,384]{3,2,1,0:T(8,128)S(1)} %pad_maximum_fusion, f32[8,8,30,383]{3,2,1,0:T(8,128)S(1)} %fusion.24), kind=kLoop, calls=%fused_computation.52 | loop fusion | flops 2949120 | bytes 14737920 | tf_op jit(solution)/shard_map/sub | solution.py:36
  28.3 1.2 fusion.20
  30.0 1.7 %fusion.22 = f32[8,8,28,384]{3,2,1,0:T(8,128)S(1)} fusion(f32[8,8,29,384]{3,2,1,0:T(8,128)S(1)} %fusion.23, f32[8,8,30,384]{3,2,1,0:T(8,128)S(1)} %fusion.26, f32[8,8,28,383]{3,2,1,0:T(8,128)S(1)} %fusion.20), kind=kLoop, calls=%fused_computation.44 | loop fusion | flops 2752512 | bytes 13755392 | tf_op jit(solution)/shard_map/sub | solution.py:36
  31.7 1.2 fusion.16
  33.5 1.7 %fusion.18 = f32[8,8,26,384]{3,2,1,0:T(8,128)S(1)} fusion(f32[8,8,27,384]{3,2,1,0:T(8,128)S(1)} %fusion.19, f32[8,8,28,384]{3,2,1,0:T(8,128)S(1)} %fusion.22, f32[8,8,26,383]{3,2,1,0:T(8,128)S(1)} %fusion.16), kind=kLoop, calls=%fused_computation.36 | loop fusion | flops 2555904 | bytes 12772864 | tf_op jit(solution)/shard_map/sub | solution.py:36
  36.2 1.1 fusion.32
  37.3 1.2 fusion.34
  38.9 1.3 %fusion = f32[2,8,24,384]{3,2,1,0:T(8,128)} fusion(bf16[2,8,8,24,384]{4,3,2,1,0:T(8,128)(2,1)S(1)} %copy-done.1, f32[8,8,24,384]{3,2,1,0:T(8,128)S(1)} %fusion.34), kind=kLoop, calls=%fused_computation.2 | loop fusion | flops 3391488 | bytes 5308416 | tf_op jit(solution)/shard_map/reduce_sum | solution.py:44
  40.3 42.5 %all-reduce.18.cloned.1.call-done = f32[2,8,24,384]{3,2,1,0:T(8,128)} async-done(((f32[2,8,24,384]{3,2,1,0:T(8,128)}), f32[2,8,24,384]{3,2,1,0:T(8,128)}) %all-reduce.18.cloned.1.call-update) | async-done | bytes 589840 | tf_op jit(solution)/shard_map/psum | solution.py:45
  82.8 1.6 %subtract_multiply_fusion = f32[2,8,24,384]{3,2,1,0:T(8,128)S(1)} fusion(f32[2,8,24,384]{3,2,1,0:T(8,128)} %param.8, f32[2,8,24,384]{3,2,1,0:T(8,128)} %all-reduce.18.cloned.1.call-done, f32[2,8,24,384]{3,2,1,0:T(8,128)} %param.7), kind=kLoop, calls=%fused_computation.72 | loop fusion | flops 294912 | bytes 2359296 | tf_op jit(solution)/shard_map/mul | solution.py:46
  85.8 2.7 %collective-permute-start.5 = (f32[8,8,4,384]{3,1,2,0:T(8,128)S(1)}, f32[8,8,4,384]{3,1,2,0:T(8,128)S(1)}, u32[]{:S(2)}, u32[]{:S(2)}) collective-permute-start(f32[8,8,4,384]{3,1,2,0:T(8,128)S(1)} %copy.26), channel_id=1, source_target_pairs={{1,0},{2,1},{3,2},{4,3},{5,4},{6,5},{7,6},{0,7},{9,8},{10,9},{11,1... | collective-permute-start | bytes 1179656 | tf_op jit(solution)/shard_map/ppermute | solution.py:18
  88.5 7.7 %collective-permute-done.4 = f32[8,8,4,384]{3,1,2,0:T(8,128)S(1)} collective-permute-done((f32[8,8,4,384]{3,1,2,0:T(8,128)S(1)}, f32[8,8,4,384]{3,1,2,0:T(8,128)S(1)}, u32[]{:S(2)}, u32[]{:S(2)}) %collective-permute-start.4) | collective-permute-done | bytes 393248 | tf_op jit(solution)/shard_map/ppermute | solution.py:16
  97.4 1.2 fusion.11
  99.2 1.7 %fusion.13 = f32[8,8,30,384]{3,2,1,0:T(8,128)S(1)} fusion(f32[8,8,31,384]{3,2,1,0:T(8,128)S(1)} %fusion.14, f32[8,8,32,384]{3,2,1,0:T(8,128)S(1)} %pad_maximum_fusion.1, f32[8,8,30,383]{3,2,1,0:T(8,128)S(1)} %fusion.11), kind=kLoop, calls=%fused_computation.26 | loop fusion | flops 2949120 | bytes 14737920 | tf_op jit(solution)/shard_map/sub | solution.py:36
  100.9 1.2 fusion.7
  102.6 1.7 %fusion.9 = f32[8,8,28,384]{3,2,1,0:T(8,128)S(1)} fusion(f32[8,8,29,384]{3,2,1,0:T(8,128)S(1)} %fusion.10, f32[8,8,30,384]{3,2,1,0:T(8,128)S(1)} %fusion.13, f32[8,8,28,383]{3,2,1,0:T(8,128)S(1)} %fusion.7), kind=kLoop, calls=%fused_computation.18 | loop fusion | flops 2752512 | bytes 13755392 | tf_op jit(solution)/shard_map/sub | solution.py:36
  104.3 1.2 fusion.3
  106.1 1.7 %fusion.5 = f32[8,8,26,384]{3,2,1,0:T(8,128)S(1)} fusion(f32[8,8,27,384]{3,2,1,0:T(8,128)S(1)} %fusion.6, f32[8,8,28,384]{3,2,1,0:T(8,128)S(1)} %fusion.9, f32[8,8,26,383]{3,2,1,0:T(8,128)S(1)} %fusion.3), kind=kLoop, calls=%fused_computation.10 | loop fusion | flops 2555904 | bytes 12772864 | tf_op jit(solution)/shard_map/sub | solution.py:36
  108.8 0.9 fusion.28
  109.7 2.9 %fusion.31 = f32[8,8,24,384]{3,2,1,0:T(8,128)} fusion(f32[8,8,24,384]{3,2,1,0:T(8,128)S(1)} %copy-done, f32[8,8,25,384]{3,2,1,0:T(8,128)S(1)} %fusion.2, f32[8,8,26,384]{3,2,1,0:T(8,128)S(1)} %fusion.5, f32[8,8,24,383]{3,2,1,0:T(8,128)S(1)} %fusion.28), kind=kLoop, calls=%fused_computation.63 | loop fusion | flops 2949120 | bytes 14149632 | tf_op jit(solution)/shard_map/add | solution.py:50
  112.6 0.8 copy.32
  (67 shorter events, 9.8 us)
Async XLA Ops:
  7.2 9.0 %copy-start.3 = (f32[2,8,24,384]{3,2,1,0:T(8,128)S(1)}, f32[2,8,24,384]{3,2,1,0:T(8,128)}, u32[]{:S(2)}) copy-start(f32[2,8,24,384]{3,2,1,0:T(8,128)} %param.9) | copy-start | bytes 1769476
  7.2 75.6 %all-reduce.18.cloned.1.call-start = ((), (), s32[]{:S(2)}) async-start(), calls=%async_computation | async-start | bytes 1179648 | tf_op jit(solution)/shard_map/psum | solution.py:45
  8.3 8.6 %collective-permute-start.2 = (f32[2,8,4,384]{3,2,1,0:T(4,128)S(1)}, f32[2,8,4,384]{3,2,1,0:T(4,128)S(1)}, u32[]{:S(2)}, u32[]{:S(2)}) collective-permute-start(f32[2,8,4,384]{3,2,1,0:T(4,128)S(1)} %get-tuple-element.8), channel_id=1, source_target_pairs={{0,1},{1,2},{2,3},{3,4},{4,5},{5,6},{6,7},{7,0},{8,9},{9,10},{10,1... | collective-permute-start | bytes 294920 | tf_op jit(solution)/shard_map/ppermute | solution.py:16
  8.9 8.0 %collective-permute-start.3 = (f32[2,8,4,384]{3,2,1,0:T(4,128)S(1)}, f32[2,8,4,384]{3,2,1,0:T(4,128)S(1)}, u32[]{:S(2)}, u32[]{:S(2)}) collective-permute-start(f32[2,8,4,384]{3,2,1,0:T(4,128)S(1)} %get-tuple-element.9), channel_id=1, source_target_pairs={{1,0},{2,1},{3,2},{4,3},{5,4},{6,5},{7,6},{0,7},{9,8},{10,9},{11,1... | collective-permute-start | bytes 294920 | tf_op jit(solution)/shard_map/ppermute | solution.py:18
  13.4 10.6 %collective-permute-start = (f32[8,8,4,384]{3,1,2,0:T(8,128)S(1)}, f32[8,8,4,384]{3,1,2,0:T(8,128)S(1)}, u32[]{:S(2)}, u32[]{:S(2)}) collective-permute-start(f32[8,8,4,384]{3,1,2,0:T(8,128)S(1)} %copy.29), channel_id=1, source_target_pairs={{0,1},{1,2},{2,3},{3,4},{4,5},{5,6},{6,7},{7,0},{8,9},{9,10},{10,1... | collective-permute-start | bytes 1179656 | tf_op jit(solution)/shard_map/ppermute | solution.py:16
  13.5 10.7 %collective-permute-start.1 = (f32[8,8,4,384]{3,1,2,0:T(8,128)S(1)}, f32[8,8,4,384]{3,1,2,0:T(8,128)S(1)}, u32[]{:S(2)}, u32[]{:S(2)}) collective-permute-start(f32[8,8,4,384]{3,1,2,0:T(8,128)S(1)} %copy.30), channel_id=1, source_target_pairs={{1,0},{2,1},{3,2},{4,3},{5,4},{6,5},{7,6},{0,7},{9,8},{10,9},{11,1... | collective-permute-start | bytes 1179656 | tf_op jit(solution)/shard_map/ppermute | solution.py:18
  17.1 7.7 %copy-start.12 = (f32[8,30,384]{2,1,0:T(8,128)}, f32[8,30,384]{2,1,0:T(8,128)S(1)}, u32[]{:S(2)}) copy-start(f32[8,30,384]{2,1,0:T(8,128)S(1)} %slice_bitcast_fusion.4) | copy-start | bytes 1105924
  17.1 7.2 %copy-start = (f32[8,8,24,384]{3,2,1,0:T(8,128)S(1)}, f32[8,8,24,384]{3,2,1,0:T(8,128)}, u32[]{:S(2)}) copy-start(f32[8,8,24,384]{3,2,1,0:T(8,128)} %param.5) | copy-start | bytes 7077892
  17.1 8.8 %copy-start.10 = (f32[8,31,384]{2,1,0:T(8,128)}, f32[8,31,384]{2,1,0:T(8,128)S(1)}, u32[]{:S(2)}) copy-start(f32[8,31,384]{2,1,0:T(8,128)S(1)} %slice_bitcast_fusion.5) | copy-start | bytes 1142788
  26.5 1.7 %copy-start.9 = (f32[8,28,384]{2,1,0:T(8,128)S(1)}, f32[8,28,384]{2,1,0:T(8,128)}, u32[]{:S(2)}) copy-start(f32[8,28,384]{2,1,0:T(8,128)} %slice_bitcast_fusion.2) | copy-start | bytes 1032196
  28.2 1.2 %copy-start.7 = (f32[8,29,384]{2,1,0:T(8,128)S(1)}, f32[8,29,384]{2,1,0:T(8,128)}, u32[]{:S(2)}) copy-start(f32[8,29,384]{2,1,0:T(8,128)} %slice_bitcast_fusion.3) | copy-start | bytes 1069060
  30.0 1.7 %copy-start.4 = (f32[8,26,384]{2,1,0:T(8,128)S(1)}, f32[8,26,384]{2,1,0:T(8,128)}, u32[]{:S(2)}) copy-start(f32[8,26,384]{2,1,0:T(8,128)} %slice_bitcast_fusion) | copy-start | bytes 958468
  31.7 1.2 copy-start.5
  35.2 1.0 copy-start.14
  37.2 1.7 %copy-start.1 = (bf16[2,8,8,24,384]{4,3,2,1,0:T(8,128)(2,1)S(1)}, bf16[2,8,8,24,384]{4,3,2,1,0:T(8,128)(2,1)}, u32[]{:S(2)}) copy-start(bf16[2,8,8,24,384]{4,3,2,1,0:T(8,128)(2,1)} %param.6) | copy-start | bytes 7077892
  82.8 2.2 %copy-start.2 = (bf16[2,8,8,24,384]{4,3,2,1,0:T(8,128)(2,1)S(1)}, bf16[2,8,8,24,384]{4,3,2,1,0:T(8,128)(2,1)}, u32[]{:S(2)}) copy-start(bf16[2,8,8,24,384]{4,3,2,1,0:T(8,128)(2,1)} %param.6) | copy-start | bytes 7077892
  85.7 10.5 %collective-permute-start.4 = (f32[8,8,4,384]{3,1,2,0:T(8,128)S(1)}, f32[8,8,4,384]{3,1,2,0:T(8,128)S(1)}, u32[]{:S(2)}, u32[]{:S(2)}) collective-permute-start(f32[8,8,4,384]{3,1,2,0:T(8,128)S(1)} %copy.25), channel_id=1, source_target_pairs={{0,1},{1,2},{2,3},{3,4},{4,5},{5,6},{6,7},{7,0},{8,9},{9,10},{10,1... | collective-permute-start | bytes 1179656 | tf_op jit(solution)/shard_map/ppermute | solution.py:16
  85.8 10.5 %collective-permute-start.5 = (f32[8,8,4,384]{3,1,2,0:T(8,128)S(1)}, f32[8,8,4,384]{3,1,2,0:T(8,128)S(1)}, u32[]{:S(2)}, u32[]{:S(2)}) collective-permute-start(f32[8,8,4,384]{3,1,2,0:T(8,128)S(1)} %copy.26), channel_id=1, source_target_pairs={{1,0},{2,1},{3,2},{4,3},{5,4},{6,5},{7,6},{0,7},{9,8},{10,9},{11,1... | collective-permute-start | bytes 1179656 | tf_op jit(solution)/shard_map/ppermute | solution.py:18
  96.4 1.0 copy-start.13
  97.4 1.2 copy-start.11
  100.9 1.2 %copy-start.8 = (f32[8,29,384]{2,1,0:T(8,128)S(1)}, f32[8,29,384]{2,1,0:T(8,128)}, u32[]{:S(2)}) copy-start(f32[8,29,384]{2,1,0:T(8,128)} %slice_bitcast_fusion.3) | copy-start | bytes 1069060
  104.3 1.2 copy-start.6
  107.8 1.0 copy-start.15
  109.7 2.9 %copy-start.16 = (f32[2,8,24,384]{3,2,1,0:T(8,128)S(1)}, f32[2,8,24,384]{3,2,1,0:T(8,128)}, u32[]{:S(2)}) copy-start(f32[2,8,24,384]{3,2,1,0:T(8,128)} %all-reduce.18.cloned.1.call-done) | copy-start | bytes 1769476
Sparse Core Ops, SparseCore 0:
  40.4 42.3 all-reduce.17
where the time goes:
time: 122 us; the launch traced here: 120 us
  waiting for transfers between devices  54 us (44%)
  other arithmetic  32.3 us (26%)
  between operations  14.5 us (12%)
  local copies, waits for them, and re-layouts  10.5 us (9%)
  starting transfers between devices  8.99 us (7%)
    psum x1, waiting for transfers between devices, per_device(): increment = lax.psum(partial_sum, 'mem')  42.5 us
    sub x7, other arithmetic, diffuse(): interior + zonal_flux[:, :, 1:] - zonal_flux[:, :, :-1] + north_flux  11.5 us
    ppermute x3, waiting for transfers between devices, extended(): lax.ppermute(tail, axis, [(i, (i + 1) % count) for i in range(count)])  11.4 us
    mul x8, other arithmetic, diffuse(): merid_face[:, :, :-1] * (interior[:, :, :, 1:] - interior[:, :, :, :-1])  9.07 us
    ppermute x3, starting transfers between devices, extended(): lax.ppermute(head, axis, [((i + 1) % count, i) for i in range(count)])  8.29 us
    mul x9, other arithmetic, diffuse(): zonal_flux = zonal_face * (field[:, :, 1:] - field[:, :, :-1])  4.23 us
    unnamed x37, local copies, waits for them, and re-layouts  3.28 us
    add x1, other arithmetic, per_device(): gradient = alpha + adjoint_field  2.88 us
  transfers between devices with their start and end apart: 7, of which 3 were waited for; matrix products, arithmetic and copies ran while one was open for 5% of the time, Pallas kernels for 0%

commit v1 on v0

v1 whole, which is shorter than its diff:
```python
import functools

import jax
import jax.numpy as jnp
from jax import lax
from jax.experimental import pallas as pl
from jax.experimental.pallas import tpu as pltpu
from jax.sharding import PartitionSpec as P

STEPS = 4
LAG_PAIR, LAG_TOTAL, LAG_PROJECT, LAG_ADJOINT = 1, 2, 4, 6
MESH = pl.DeviceIdType.MESH


def diffuse(field, zonal, merid):
    columns, rows = field.shape
    for _ in range(STEPS):
        zonal_flux = zonal * (pltpu.roll(field, columns - 1, 0) - field)
        merid_flux = merid * (pltpu.roll(field, rows - 1, 1) - field)
        field = (
            (field + zonal_flux)
            - pltpu.roll(zonal_flux, 1, 0)
            + (merid_flux - pltpu.roll(merid_flux, 1, 1))
        )
    return field


def kernel(
    tiles, alpha, ens, innov, prec, diff, grad, inc,
    av, ev, iv, pv, dv, pj, part, r1, r2, tot,
    a_send, a_recv, d_send, d_recv, p_send, p_recv,
    r1_send, r1_recv, r2_send, r2_recv, t_send, t_recv,
    a_sem, e_sem, d_sem, i_sem, w_sem, g_sem, n_sem,
):
    members, levels, cols, rows = alpha.shape
    z = lax.axis_index("mem")
    t = lax.axis_index("tile")
    right, left = lax.rem(t + 1, tiles), lax.rem(t + tiles - 1, tiles)
    inner = (z == 1) | (z == 2)
    outer = (z == 0) | (z == 3)
    partner = z + 1 - 2 * lax.rem(z, 2)
    across = 3 - z

    def remote(src, dst, send, recv, where):
        return pltpu.make_async_remote_copy(
            src_ref=src, dst_ref=dst, send_sem=send, recv_sem=recv,
            device_id=where, device_id_type=MESH,
        )

    def halo(src, dst, send, recv, l):
        return (
            remote(src.at[:, l, 0:STEPS], dst.at[:, l, cols:cols + STEPS],
                   send.at[0, l], recv.at[0, l], {"tile": left}),
            remote(src.at[:, l, cols - STEPS:cols], dst.at[:, l, cols + STEPS:cols + 2 * STEPS],
                   send.at[1, l], recv.at[1, l], {"tile": right}),
        )

    def alpha_halo(l):
        return halo(alpha, av, a_send, a_recv, l)

    def diff_halo(l):
        return halo(diff, dv, d_send, d_recv, l)

    def proj_halo(l):
        return halo(pj, pj, p_send, p_recv, l)

    def local(l):
        return (
            pltpu.make_async_copy(diff.at[:, l], dv.at[:, l, 0:cols], d_sem.at[l]),
            pltpu.make_async_copy(alpha.at[:, l], av.at[:, l, 0:cols], a_sem.at[l]),
            pltpu.make_async_copy(ens.at[:, :, l], ev.at[:, :, l], e_sem.at[l]),
        )

    def to_inner(l):
        return remote(part.at[l], r1.at[l], r1_send.at[l], r1_recv.at[l], {"mem": partner})

    def to_across(l):
        return remote(part.at[l], r2.at[l], r2_send.at[l], r2_recv.at[l], {"mem": across})

    def to_outer(l):
        return remote(tot.at[l], tot.at[l], t_send.at[l], t_recv.at[l], {"mem": partner})

    def out_grad(l):
        return pltpu.make_async_copy(av.at[:, l, 0:cols], grad.at[:, l], g_sem.at[l])

    def out_inc(l):
        return pltpu.make_async_copy(tot.at[l], inc.at[:, l], n_sem.at[l])

    innov_copy = pltpu.make_async_copy(innov, iv, i_sem)
    prec_copy = pltpu.make_async_copy(prec, pv, w_sem)

    barrier = pltpu.get_barrier_semaphore()
    for where in ({"tile": left}, {"tile": right}):
        pl.semaphore_signal(barrier, inc=1, device_id=where, device_id_type=MESH)
    for step in range(1, 4):
        pl.semaphore_signal(
            barrier, inc=1, device_id={"mem": lax.rem(z + step, 4)}, device_id_type=MESH
        )

    def load(l, carry):
        for copy in local(l):
            copy.start()
        return carry

    lax.fori_loop(0, levels, load, 0)
    innov_copy.start()
    prec_copy.start()
    pl.semaphore_wait(barrier, 5)

    def send_first(l, carry):
        for copy in diff_halo(l) + alpha_halo(l):
            copy.start()
        return carry

    lax.fori_loop(0, levels, send_first, 0)

    def coefficients(l):
        zonal, merid = dv[0, l], dv[1, l]
        lane = lax.broadcasted_iota(jnp.int32, merid.shape, 1)
        return zonal, jnp.where(lane < rows - 1, merid, 0.0)

    def forward(l):
        for copy in local(l):
            copy.wait()
        for copy in diff_halo(l) + alpha_halo(l):
            copy.wait_recv()
        zonal, merid = coefficients(l)
        part[l] = jnp.zeros(part.shape[1:], jnp.float32)

        def member(k, carry):
            localized = diffuse(av[k, l], zonal, merid)[0:cols]
            for slot in range(2):
                part[l, slot] += ev[slot, k, l].astype(jnp.float32) * localized
            return carry

        lax.fori_loop(0, members, member, 0)

        @pl.when(outer)
        def _():
            to_inner(l).start()

    def pair(l):
        @pl.when(inner)
        def _():
            to_inner(l).wait_recv()
            part[l] += r1[l]
            to_across(l).start()

    def total(l):
        @pl.when(inner)
        def _():
            to_across(l).wait_recv()
            tot[l] = part[l] + r2[l]
            to_outer(l).start()

    def project(l):
        @pl.when(outer)
        def _():
            to_outer(l).wait_recv()

        out_inc(l).start()
        weighted = [pv[slot, l] * (tot[l, slot] - iv[slot, l]) for slot in range(2)]

        def member(k, carry):
            pj[k, l, 0:cols] = (
                ev[0, k, l].astype(jnp.float32) * weighted[0]
                + ev[1, k, l].astype(jnp.float32) * weighted[1]
            )
            return carry

        lax.fori_loop(0, members, member, 0)
        for copy in proj_halo(l):
            copy.start()

    def adjoint(l):
        for copy in proj_halo(l):
            copy.wait_recv()
        zonal, merid = coefficients(l)

        def member(k, carry):
            av[k, l, 0:cols] += diffuse(pj[k, l], zonal, merid)[0:cols]
            return carry

        lax.fori_loop(0, members, member, 0)
        out_grad(l).start()

    def stage(work, step, lag):
        l = step - lag

        @pl.when((l >= 0) & (l < levels))
        def _():
            work(l)

    def step(s, carry):
        @pl.when(s == LAG_PROJECT)
        def _():
            innov_copy.wait()
            prec_copy.wait()

        stage(forward, s, 0)
        stage(pair, s, LAG_PAIR)
        stage(total, s, LAG_TOTAL)
        stage(project, s, LAG_PROJECT)
        stage(adjoint, s, LAG_ADJOINT)
        return carry

    lax.fori_loop(0, levels + LAG_ADJOINT, step, 0)

    def drain(l, carry):
        for copy in diff_halo(l) + alpha_halo(l) + proj_halo(l):
            copy.wait_send()

        @pl.when(outer)
        def _():
            to_inner(l).wait_send()

        @pl.when(inner)
        def _():
            to_across(l).wait_send()
            to_outer(l).wait_send()

        out_grad(l).wait()
        out_inc(l).wait()
        return carry

    lax.fori_loop(0, levels, drain, 0)


def per_device(tiles, alpha, ensemble, innovation, precision, diffusivity):
    members, levels, cols, rows = alpha.shape
    wide = cols + 2 * STEPS
    f32 = jnp.float32
    dma = pltpu.SemaphoreType.DMA
    slot = pltpu.VMEM((levels, 2, cols, rows), f32)
    return pl.pallas_call(
        functools.partial(kernel, tiles),
        out_shape=(
            jax.ShapeDtypeStruct(alpha.shape, f32),
            jax.ShapeDtypeStruct(innovation.shape, f32),
        ),
        in_specs=[pl.BlockSpec(memory_space=pl.ANY)] * 5,
        out_specs=(pl.BlockSpec(memory_space=pl.ANY), pl.BlockSpec(memory_space=pl.ANY)),
        scratch_shapes=[
            pltpu.VMEM((members, levels, wide, rows), f32),
            pltpu.VMEM(ensemble.shape, ensemble.dtype),
            pltpu.VMEM(innovation.shape, f32),
            pltpu.VMEM(precision.shape, f32),
            pltpu.VMEM((2, levels, wide, rows), f32),
            pltpu.VMEM((members, levels, wide, rows), f32),
            slot, slot, slot, slot,
            *[dma((2, levels))] * 6,
            *[dma((levels,))] * 6,
            *[dma((levels,))] * 3,
            dma, dma,
            dma((levels,)), dma((levels,)),
        ],
        compiler_params=pltpu.CompilerParams(collective_id=0, has_side_effects=True),
    )(alpha, ensemble, innovation, precision, diffusivity)


def solution(mesh):
    assert mesh.shape["mem"] == 4
    in_specs = (
        P("mem", None, "tile", None),
        P(None, "mem", None, "tile", None),
        P(None, None, "tile", None),
        P(None, None, "tile", None),
        P(None, None, "tile", None),
    )
    out_specs = (P("mem", None, "tile", None), P(None, None, "tile", None))
    return jax.shard_map(
        functools.partial(per_device, mesh.shape["tile"]),
        mesh=mesh, in_specs=in_specs, out_specs=out_specs, check_vma=False,
    )
```

time: 122 us -> 96 us (0.79)
  Pallas kernels: 0 us -> 90.6 us
  waiting for transfers between devices: 54 us -> 0 us
  other arithmetic: 32.3 us -> 0 us
  between operations: 14.5 us -> 0.65 us
  starting transfers between devices: 8.99 us -> 0 us
  local copies, waits for them, and re-layouts: 10.5 us -> 4.12 us
    pallas_call x0 -> x1, Pallas kernels: none -> 90.6 us  [per_device(): pl.pallas_call(functools.partial(kernel, tiles), out_shape=(jax.ShapeDtyp...]
    psum x1 -> x0, waiting for transfers between devices: 42.5 us -> none  [per_device(): increment = lax.psum(partial_sum, 'mem')]
    mul x18 -> x0, other arithmetic: 15 us -> none  [the longest x8 9.07 us: diffuse(): merid_face[:, :, :-1] * (interior[:, :, :, 1:] - interior[:, :, :, :-1])]
    sub x7 -> x0, other arithmetic: 11.5 us -> none  [diffuse(): interior + zonal_flux[:, :, 1:] - zonal_flux[:, :, :-1] + north_flux]
    ppermute x6 -> x0, waiting for transfers between devices: 11.4 us -> none  [the longest x3 11.4 us: extended(): lax.ppermute(tail, axis, [(i, (i + 1) % count) for i in range(count)])]
    ppermute x6 -> x0, starting transfers between devices: 8.95 us -> none  [the longest x3 8.29 us: extended(): lax.ppermute(head, axis, [((i + 1) % count, i) for i in range(count)])]
    add x1 -> x0, other arithmetic: 2.88 us -> none  [per_device(): gradient = alpha + adjoint_field]
    slice x5 -> x0, local copies, waits for them, and re-layouts: 2.85 us -> none  [the longest x4 2.83 us: extended(): lax.slice_in_dim(cells, cells.shape[dim] - width, cells.shape[dim], axis=...]
  transfers between devices with their start and end apart: 7 -> 0, of which waited for: 3 -> 0; matrix products, arithmetic and copies ran while one was open for 5% -> 0% of each run, Pallas kernels for 0% -> 0%
where the time goes in v1:
time: 96 us; the launch traced here: 95.4 us
  Pallas kernels  90.6 us (94%)
  local copies, waits for them, and re-layouts  4.12 us (4%)
    pallas_call x1, Pallas kernels, per_device(): pl.pallas_call(functools.partial(kernel, tiles), out_shape=(jax.ShapeDtyp...  90.6 us
    unnamed x4, local copies, waits for them, and re-layouts  4.12 us

profile of v1, /device:TPU:0, one launch (start us, length us, event | category | flops | bytes accessed | tf_op | source)
XLA Modules:
  0.0 95.4 jit_solution(15344549776070224951)
XLA Ops:
  0.6 90.6 %shard_map.68 = (f32[8,8,24,384]{3,2,1,0:T(8,128)}, f32[2,8,24,384]{3,2,1,0:T(8,128)}) custom-call(f32[8,8,24,384]{3,2,1,0:T(8,128)} %alpha.1, bf16[2,8,8,24,384]{4,3,2,1,0:T(8,128)(2,1)} %ens.1, f32[2,8,24,384]{3,2,1,0:T(8,128)} %innov.1, f32[2,8,24,384]{3,2,1,0:T(8,128)} %prec.1, f32[2,8,24,384]{3,2,1,0:T(8,128)} %diff.1), custom_call_target="tpu_custom_call" | custom-call | tf_op jit(solution)/shard_map/pallas_call | solution.py:235
  91.3 0.0 copy-start
  91.3 3.3 %copy.9 = f32[8,8,24,384]{3,2,1,0:T(8,128)} copy(f32[8,8,24,384]{3,2,1,0:T(8,128)} %get-tuple-element.4) | data formatting | bytes 4718592
  94.6 0.0 copy-done
  94.6 0.8 copy.10
Async XLA Ops:
  91.3 3.3 %copy-start = (f32[2,8,24,384]{3,2,1,0:T(8,128)S(1)}, f32[2,8,24,384]{3,2,1,0:T(8,128)}, u32[]{:S(2)}) copy-start(f32[2,8,24,384]{3,2,1,0:T(8,128)} %get-tuple-element.5) | copy-start | bytes 1769476

commit v2 on v1

--- a/solution.py
+++ b/solution.py
@@ -8,26 +8,26 @@
 from jax.sharding import PartitionSpec as P
 
 STEPS = 4
+UNROLL = 2
 LAG_PAIR, LAG_TOTAL, LAG_PROJECT, LAG_ADJOINT = 1, 2, 4, 6
 MESH = pl.DeviceIdType.MESH
 
 
-def diffuse(field, zonal, merid):
-    columns, rows = field.shape
+def diffuse(field, center, east, west, north, south):
+    columns, rows = field.shape[-2:]
+    lead = field.ndim - 2
     for _ in range(STEPS):
-        zonal_flux = zonal * (pltpu.roll(field, columns - 1, 0) - field)
-        merid_flux = merid * (pltpu.roll(field, rows - 1, 1) - field)
         field = (
-            (field + zonal_flux)
-            - pltpu.roll(zonal_flux, 1, 0)
-            + (merid_flux - pltpu.roll(merid_flux, 1, 1))
+            center * field
+            + (east * pltpu.roll(field, columns - 1, lead) + west * pltpu.roll(field, 1, lead))
+            + (north * pltpu.roll(field, rows - 1, lead + 1) + south * pltpu.roll(field, 1, lead + 1))
         )
     return field
 
 
 def kernel(
     tiles, alpha, ens, innov, prec, diff, grad, inc,
-    av, ev, iv, pv, dv, pj, part, r1, r2, tot,
+    av, ev, iv, pv, dv, pj, part, r1, r2, tot, cf,
     a_send, a_recv, d_send, d_recv, p_send, p_recv,
     r1_send, r1_recv, r2_send, r2_recv, t_send, t_recv,
     a_sem, e_sem, d_sem, i_sem, w_sem, g_sem, n_sem,
@@ -115,25 +115,34 @@
     lax.fori_loop(0, levels, send_first, 0)
 
     def coefficients(l):
-        zonal, merid = dv[0, l], dv[1, l]
+        east, merid = dv[0, l], dv[1, l]
         lane = lax.broadcasted_iota(jnp.int32, merid.shape, 1)
-        return zonal, jnp.where(lane < rows - 1, merid, 0.0)
+        north = jnp.where(lane < rows - 1, merid, 0.0)
+        west, south = pltpu.roll(east, 1, 0), pltpu.roll(north, 1, 1)
+        cf[0] = 1.0 - ((east + west) + (north + south))
+        cf[1], cf[2], cf[3], cf[4] = east, west, north, south
+
+    def spread(field):
+        return diffuse(field, *[cf[i] for i in range(5)])
 
     def forward(l):
         for copy in local(l):
             copy.wait()
         for copy in diff_halo(l) + alpha_halo(l):
             copy.wait_recv()
-        zonal, merid = coefficients(l)
+        coefficients(l)
         part[l] = jnp.zeros(part.shape[1:], jnp.float32)
 
         def member(k, carry):
-            localized = diffuse(av[k, l], zonal, merid)[0:cols]
+            localized = [spread(av[k * UNROLL + i, l])[0:cols] for i in range(UNROLL)]
             for slot in range(2):
-                part[l, slot] += ev[slot, k, l].astype(jnp.float32) * localized
+                part[l, slot] += sum(
+                    ev[slot, k * UNROLL + i, l].astype(jnp.float32) * localized[i]
+                    for i in range(UNROLL)
+                )
             return carry
 
-        lax.fori_loop(0, members, member, 0)
+        lax.fori_loop(0, members // UNROLL, member, 0)
 
         @pl.when(outer)
         def _():
@@ -175,13 +184,15 @@
     def adjoint(l):
         for copy in proj_halo(l):
             copy.wait_recv()
-        zonal, merid = coefficients(l)
+        coefficients(l)
 
         def member(k, carry):
-            av[k, l, 0:cols] += diffuse(pj[k, l], zonal, merid)[0:cols]
+            moved = [spread(pj[k * UNROLL + i, l])[0:cols] for i in range(UNROLL)]
+            for i in range(UNROLL):
+                av[k * UNROLL + i, l, 0:cols] += moved[i]
             return carry
 
-        lax.fori_loop(0, members, member, 0)
+        lax.fori_loop(0, members // UNROLL, member, 0)
         out_grad(l).start()
 
     def stage(work, step, lag):
@@ -248,6 +259,7 @@
             pltpu.VMEM((2, levels, wide, rows), f32),
             pltpu.VMEM((members, levels, wide, rows), f32),
             slot, slot, slot, slot,
+            pltpu.VMEM((5, wide, rows), f32),
             *[dma((2, levels))] * 6,
             *[dma((levels,))] * 6,
             *[dma((levels,))] * 3,

time: 96 us -> 53.6 us (0.56)
  Pallas kernels: 90.6 us -> 48.7 us
    pallas_call x1, Pallas kernels: 90.6 us -> 48.7 us  [per_device(): pl.pallas_call(functools.partial(kernel, tiles), out_shape=(jax.ShapeDtyp...]
where the time goes in v2:
time: 53.6 us; the launch traced here: 53.4 us
  Pallas kernels  48.7 us (91%)
  local copies, waits for them, and re-layouts  4.12 us (8%)
  between operations  0.65 us (1%)
    pallas_call x1, Pallas kernels, per_device(): pl.pallas_call(functools.partial(kernel, tiles), out_shape=(jax.ShapeDtyp...  48.7 us
    unnamed x4, local copies, waits for them, and re-layouts  4.12 us

profile of v2, /device:TPU:0, one launch (start us, length us, event | category | flops | bytes accessed | tf_op | source)
XLA Modules:
  0.0 53.4 jit_solution(481090185551458717)
XLA Ops:
  0.6 48.7 %shard_map.68 = (f32[8,8,24,384]{3,2,1,0:T(8,128)}, f32[2,8,24,384]{3,2,1,0:T(8,128)}) custom-call(f32[8,8,24,384]{3,2,1,0:T(8,128)} %alpha.1, bf16[2,8,8,24,384]{4,3,2,1,0:T(8,128)(2,1)} %ens.1, f32[2,8,24,384]{3,2,1,0:T(8,128)} %innov.1, f32[2,8,24,384]{3,2,1,0:T(8,128)} %prec.1, f32[2,8,24,384]{3,2,1,0:T(8,128)} %diff.1), custom_call_target="tpu_custom_call" | custom-call | tf_op jit(solution)/shard_map/pallas_call | solution.py:246
  49.3 0.0 copy-start
  49.3 3.3 %copy.9 = f32[8,8,24,384]{3,2,1,0:T(8,128)} copy(f32[8,8,24,384]{3,2,1,0:T(8,128)} %get-tuple-element.4) | data formatting | bytes 4718592
  52.6 0.0 copy-done
  52.6 0.8 %copy.10 = f32[2,8,24,384]{3,2,1,0:T(8,128)} copy(f32[2,8,24,384]{3,2,1,0:T(8,128)S(1)} %copy-done) | data formatting | bytes 1179648
Async XLA Ops:
  49.3 3.3 %copy-start = (f32[2,8,24,384]{3,2,1,0:T(8,128)S(1)}, f32[2,8,24,384]{3,2,1,0:T(8,128)}, u32[]{:S(2)}) copy-start(f32[2,8,24,384]{3,2,1,0:T(8,128)} %get-tuple-element.5) | copy-start | bytes 1769476

commit v3 on v2

--- a/solution.py
+++ b/solution.py
@@ -8,8 +8,8 @@
 from jax.sharding import PartitionSpec as P
 
 STEPS = 4
-UNROLL = 2
-LAG_PAIR, LAG_TOTAL, LAG_PROJECT, LAG_ADJOINT = 1, 2, 4, 6
+UNROLL = 4
+LAG_PAIR, LAG_TOTAL, LAG_PROJECT, LAG_ADJOINT = 2, 4, 7, 9
 MESH = pl.DeviceIdType.MESH
 
 
@@ -30,7 +30,7 @@
     av, ev, iv, pv, dv, pj, part, r1, r2, tot, cf,
     a_send, a_recv, d_send, d_recv, p_send, p_recv,
     r1_send, r1_recv, r2_send, r2_recv, t_send, t_recv,
-    a_sem, e_sem, d_sem, i_sem, w_sem, g_sem, n_sem,
+    a_sem, e_sem, d_sem, i_sem, w_sem,
 ):
     members, levels, cols, rows = alpha.shape
     z = lax.axis_index("mem")
@@ -80,12 +80,6 @@
     def to_outer(l):
         return remote(tot.at[l], tot.at[l], t_send.at[l], t_recv.at[l], {"mem": partner})
 
-    def out_grad(l):
-        return pltpu.make_async_copy(av.at[:, l, 0:cols], grad.at[:, l], g_sem.at[l])
-
-    def out_inc(l):
-        return pltpu.make_async_copy(tot.at[l], inc.at[:, l], n_sem.at[l])
-
     innov_copy = pltpu.make_async_copy(innov, iv, i_sem)
     prec_copy = pltpu.make_async_copy(prec, pv, w_sem)
 
@@ -119,11 +113,11 @@
         lane = lax.broadcasted_iota(jnp.int32, merid.shape, 1)
         north = jnp.where(lane < rows - 1, merid, 0.0)
         west, south = pltpu.roll(east, 1, 0), pltpu.roll(north, 1, 1)
-        cf[0] = 1.0 - ((east + west) + (north + south))
-        cf[1], cf[2], cf[3], cf[4] = east, west, north, south
-
-    def spread(field):
-        return diffuse(field, *[cf[i] for i in range(5)])
+        cf[l, 0] = 1.0 - ((east + west) + (north + south))
+        cf[l, 1], cf[l, 2], cf[l, 3], cf[l, 4] = east, west, north, south
+
+    def spread(field, l):
+        return diffuse(field, *[cf[l, i] for i in range(5)])
 
     def forward(l):
         for copy in local(l):
@@ -134,7 +128,7 @@
         part[l] = jnp.zeros(part.shape[1:], jnp.float32)
 
         def member(k, carry):
-            localized = [spread(av[k * UNROLL + i, l])[0:cols] for i in range(UNROLL)]
+            localized = [spread(av[k * UNROLL + i, l], l)[0:cols] for i in range(UNROLL)]
             for slot in range(2):
                 part[l, slot] += sum(
                     ev[slot, k * UNROLL + i, l].astype(jnp.float32) * localized[i]
@@ -167,33 +161,32 @@
         def _():
             to_outer(l).wait_recv()
 
-        out_inc(l).start()
+        inc[:, l] = tot[l]
         weighted = [pv[slot, l] * (tot[l, slot] - iv[slot, l]) for slot in range(2)]
 
         def member(k, carry):
-            pj[k, l, 0:cols] = (
-                ev[0, k, l].astype(jnp.float32) * weighted[0]
-                + ev[1, k, l].astype(jnp.float32) * weighted[1]
-            )
+            for i in range(4):
+                pj[4 * k + i, l, 0:cols] = (
+                    ev[0, 4 * k + i, l].astype(jnp.float32) * weighted[0]
+                    + ev[1, 4 * k + i, l].astype(jnp.float32) * weighted[1]
+                )
             return carry
 
-        lax.fori_loop(0, members, member, 0)
+        lax.fori_loop(0, members // 4, member, 0)
         for copy in proj_halo(l):
             copy.start()
 
     def adjoint(l):
         for copy in proj_halo(l):
             copy.wait_recv()
-        coefficients(l)
 
         def member(k, carry):
-            moved = [spread(pj[k * UNROLL + i, l])[0:cols] for i in range(UNROLL)]
+            moved = [spread(pj[k * UNROLL + i, l], l)[0:cols] for i in range(UNROLL)]
             for i in range(UNROLL):
-                av[k * UNROLL + i, l, 0:cols] += moved[i]
+                grad[k * UNROLL + i, l] = av[k * UNROLL + i, l, 0:cols] + moved[i]
             return carry
 
         lax.fori_loop(0, members // UNROLL, member, 0)
-        out_grad(l).start()
 
     def stage(work, step, lag):
         l = step - lag
@@ -208,10 +201,10 @@
             innov_copy.wait()
             prec_copy.wait()
 
-        stage(forward, s, 0)
         stage(pair, s, LAG_PAIR)
         stage(total, s, LAG_TOTAL)
         stage(project, s, LAG_PROJECT)
+        stage(forward, s, 0)
         stage(adjoint, s, LAG_ADJOINT)
         return carry
 
@@ -230,8 +223,6 @@
             to_across(l).wait_send()
             to_outer(l).wait_send()
 
-        out_grad(l).wait()
-        out_inc(l).wait()
         return carry
 
     lax.fori_loop(0, levels, drain, 0)
@@ -245,12 +236,9 @@
     slot = pltpu.VMEM((levels, 2, cols, rows), f32)
     return pl.pallas_call(
         functools.partial(kernel, tiles),
-        out_shape=(
-            jax.ShapeDtypeStruct(alpha.shape, f32),
-            jax.ShapeDtypeStruct(innovation.shape, f32),
-        ),
+        out_shape=(pltpu.VMEM(alpha.shape, f32), pltpu.VMEM(innovation.shape, f32)),
         in_specs=[pl.BlockSpec(memory_space=pl.ANY)] * 5,
-        out_specs=(pl.BlockSpec(memory_space=pl.ANY), pl.BlockSpec(memory_space=pl.ANY)),
+        out_specs=(pl.BlockSpec(memory_space=pltpu.VMEM), pl.BlockSpec(memory_space=pltpu.VMEM)),
         scratch_shapes=[
             pltpu.VMEM((members, levels, wide, rows), f32),
             pltpu.VMEM(ensemble.shape, ensemble.dtype),
@@ -259,12 +247,11 @@
             pltpu.VMEM((2, levels, wide, rows), f32),
             pltpu.VMEM((members, levels, wide, rows), f32),
             slot, slot, slot, slot,
-            pltpu.VMEM((5, wide, rows), f32),
+            pltpu.VMEM((levels, 5, wide, rows), f32),
             *[dma((2, levels))] * 6,
             *[dma((levels,))] * 6,
             *[dma((levels,))] * 3,
             dma, dma,
-            dma((levels,)), dma((levels,)),
         ],
         compiler_params=pltpu.CompilerParams(collective_id=0, has_side_effects=True),
     )(alpha, ensemble, innovation, precision, diffusivity)

time: 53.6 us -> 43.6 us (0.81)
  Pallas kernels: 48.7 us -> 40.6 us
  local copies, waits for them, and re-layouts: 4.12 us -> 2.22 us
    pallas_call x1, Pallas kernels: 48.7 us -> 40.6 us  [per_device(): pl.pallas_call(functools.partial(kernel, tiles), out_shape=(pltpu.VMEM(al...]
    unnamed x4 -> x2, local copies, waits for them, and re-layouts: 4.12 us -> 2.22 us
where the time goes in v3:
time: 43.6 us; the launch traced here: 43.5 us
  Pallas kernels  40.6 us (93%)
  local copies, waits for them, and re-layouts  2.22 us (5%)
  between operations  0.64 us (1%)
    pallas_call x1, Pallas kernels, per_device(): pl.pallas_call(functools.partial(kernel, tiles), out_shape=(pltpu.VMEM(al...  40.6 us
    unnamed x2, local copies, waits for them, and re-layouts  2.22 us

profile of v3, /device:TPU:0, one launch (start us, length us, event | category | flops | bytes accessed | tf_op | source)
XLA Modules:
  0.0 43.5 jit_solution(12852947200367459844)
XLA Ops:
  0.6 40.6 %shard_map.68 = (f32[8,8,24,384]{3,2,1,0:T(8,128)S(1)}, f32[2,8,24,384]{3,2,1,0:T(8,128)S(1)}) custom-call(f32[8,8,24,384]{3,2,1,0:T(8,128)} %alpha.1, bf16[2,8,8,24,384]{4,3,2,1,0:T(8,128)(2,1)} %ens.1, f32[2,8,24,384]{3,2,1,0:T(8,128)} %innov.1, f32[2,8,24,384]{3,2,1,0:T(8,128)} %prec.1, f32[2,8,24,384]{3,2,1,0:T(8,128)} %diff.1), custom_call_target="tpu_custom_call" | custom-call | tf_op jit(solution)/shard_map/pallas_call | solution.py:237
  41.2 1.4 %copy.9 = f32[8,8,24,384]{3,2,1,0:T(8,128)} copy(f32[8,8,24,384]{3,2,1,0:T(8,128)S(1)} %get-tuple-element.2) | data formatting | bytes 4718592
  42.7 0.8 %copy.10 = f32[2,8,24,384]{3,2,1,0:T(8,128)} copy(f32[2,8,24,384]{3,2,1,0:T(8,128)S(1)} %get-tuple-element.3) | data formatting | bytes 1179648

commit v4 on v3

--- a/solution.py
+++ b/solution.py
@@ -86,10 +86,11 @@
     barrier = pltpu.get_barrier_semaphore()
     for where in ({"tile": left}, {"tile": right}):
         pl.semaphore_signal(barrier, inc=1, device_id=where, device_id_type=MESH)
-    for step in range(1, 4):
-        pl.semaphore_signal(
-            barrier, inc=1, device_id={"mem": lax.rem(z + step, 4)}, device_id_type=MESH
-        )
+    pl.semaphore_signal(barrier, inc=1, device_id={"mem": partner}, device_id_type=MESH)
+
+    @pl.when(inner)
+    def _():
+        pl.semaphore_signal(barrier, inc=1, device_id={"mem": across}, device_id_type=MESH)
 
     def load(l, carry):
         for copy in local(l):
@@ -99,7 +100,14 @@
     lax.fori_loop(0, levels, load, 0)
     innov_copy.start()
     prec_copy.start()
-    pl.semaphore_wait(barrier, 5)
+
+    @pl.when(inner)
+    def _():
+        pl.semaphore_wait(barrier, 4)
+
+    @pl.when(outer)
+    def _():
+        pl.semaphore_wait(barrier, 3)
 
     def send_first(l, carry):
         for copy in diff_halo(l) + alpha_halo(l):
@@ -165,14 +173,14 @@
         weighted = [pv[slot, l] * (tot[l, slot] - iv[slot, l]) for slot in range(2)]
 
         def member(k, carry):
-            for i in range(4):
-                pj[4 * k + i, l, 0:cols] = (
-                    ev[0, 4 * k + i, l].astype(jnp.float32) * weighted[0]
-                    + ev[1, 4 * k + i, l].astype(jnp.float32) * weighted[1]
+            for i in range(8):
+                pj[8 * k + i, l, 0:cols] = (
+                    ev[0, 8 * k + i, l].astype(jnp.float32) * weighted[0]
+                    + ev[1, 8 * k + i, l].astype(jnp.float32) * weighted[1]
                 )
             return carry
 
-        lax.fori_loop(0, members // 4, member, 0)
+        lax.fori_loop(0, members // 8, member, 0)
         for copy in proj_halo(l):
             copy.start()
 
@@ -201,8 +209,8 @@
             innov_copy.wait()
             prec_copy.wait()
 
+        stage(total, s, LAG_TOTAL)
         stage(pair, s, LAG_PAIR)
-        stage(total, s, LAG_TOTAL)
         stage(project, s, LAG_PROJECT)
         stage(forward, s, 0)
         stage(adjoint, s, LAG_ADJOINT)

time: 43.6 us -> 42.8 us (0.982)
  Pallas kernels: 40.6 us -> 39.7 us
    pallas_call x1, Pallas kernels: 40.6 us -> 39.7 us  [per_device(): pl.pallas_call(functools.partial(kernel, tiles), out_shape=(pltpu.VMEM(al...]
where the time goes in v4:
time: 42.8 us; the launch traced here: 42.6 us
  Pallas kernels  39.7 us (93%)
  local copies, waits for them, and re-layouts  2.22 us (5%)
  between operations  0.64 us (1%)
    pallas_call x1, Pallas kernels, per_device(): pl.pallas_call(functools.partial(kernel, tiles), out_shape=(pltpu.VMEM(al...  39.7 us
    unnamed x2, local copies, waits for them, and re-layouts  2.22 us

profile of v4, /device:TPU:0, one launch (start us, length us, event | category | flops | bytes accessed | tf_op | source)
XLA Modules:
  0.0 42.6 jit_solution(11084712144690037782)
XLA Ops:
  0.6 39.7 %shard_map.68 = (f32[8,8,24,384]{3,2,1,0:T(8,128)S(1)}, f32[2,8,24,384]{3,2,1,0:T(8,128)S(1)}) custom-call(f32[8,8,24,384]{3,2,1,0:T(8,128)} %alpha.1, bf16[2,8,8,24,384]{4,3,2,1,0:T(8,128)(2,1)} %ens.1, f32[2,8,24,384]{3,2,1,0:T(8,128)} %innov.1, f32[2,8,24,384]{3,2,1,0:T(8,128)} %prec.1, f32[2,8,24,384]{3,2,1,0:T(8,128)} %diff.1), custom_call_target="tpu_custom_call" | custom-call | tf_op jit(solution)/shard_map/pallas_call | solution.py:245
  40.4 1.4 %copy.9 = f32[8,8,24,384]{3,2,1,0:T(8,128)} copy(f32[8,8,24,384]{3,2,1,0:T(8,128)S(1)} %get-tuple-element.2) | data formatting | bytes 4718592
  41.8 0.8 %copy.10 = f32[2,8,24,384]{3,2,1,0:T(8,128)} copy(f32[2,8,24,384]{3,2,1,0:T(8,128)S(1)} %get-tuple-element.3) | data formatting | bytes 1179648
